TPU v7x, 512 devices: a whole 4x4x16 slice. The times are simulated.
512 devices in a mesh: dp: 16 (over z), seq: 8 (over x, core), index: 4 (over y).
Axes of the slice: x: 4, y: 4, z: 16, core: 2. Of those that a mesh axis runs over, the one named last changes fastest.
Arguments:
- hidden: bfloat16 [16, 2048, 2048], P('dp', 'seq'), may hold values from -32 to 32
- proj_weight: bfloat16 [4, 2048, 1536], P(None, 'dp', 'index')
- stretch_lengths: int32 [16, 32], P('dp'), may hold values from 1 to 512, 2048 in all within a row
- shard_of: int32 [16, 32, 1], P('dp', 'seq'), may hold values from 0 to 3; in each aligned block of 4 rows (0 to 3, 4 to 7, ..., all dimensions but the last counted through in order) at most 2 rows name the same one
Outputs:
- layer_out: bfloat16 [16, 2048, 2048], P('dp', 'seq', 'index')
- shelf: float32 [16, 8, 4, 2, 2048], P('dp', 'seq', 'index')
Inputs may be any that keep to these rules, and one draw needn't show every extreme that they name: `stretch_lengths`: the 32 lengths of a manual sum to 2048; the largest is 512. `shard_of`: in each aligned block of 4 rows of a manual no shard is named more than 2 times, a bound that some block reaches.
All inputs are finite; a program needn't handle non-finite values.
Results may differ from a plain program's by a relative error of at most 0.01.
Values may be sent and summed in bfloat16 or wider, within the bound.
A program may use at most 64 MiB of HBM per device.

v0:
```python
import jax
import jax.numpy as jnp
from jax import lax
from jax.sharding import PartitionSpec as P

D = 2048
HD = 64
HALF_WIN = 256


def with_halo(cells, sides, width):
    for axis, dim in sides:
        count = lax.axis_size(axis)
        ends = count - 1
        head = lax.slice_in_dim(cells, 0, width, axis=dim)
        tail = lax.slice_in_dim(cells, cells.shape[dim] - width, cells.shape[dim], axis=dim)
        cells = jnp.concatenate(
            [
                lax.ppermute(tail, axis, [(i, (i + 1) % count) for i in range(ends)]),
                cells,
                lax.ppermute(head, axis, [((i + 1) % count, i) for i in range(ends)]),
            ],
            axis=dim,
        )
    return cells


def rotate(values_in, positions):
    half_dim = HD // 2
    freqs = 10000.0 ** (-2.0 * jnp.arange(half_dim, dtype=jnp.float32) / HD)
    angles = positions.astype(jnp.float32)[:, None] * freqs[None, :]
    cosine = jnp.cos(angles)[:, None, :]
    sine = jnp.sin(angles)[:, None, :]
    first = values_in[..., :half_dim]
    second = values_in[..., half_dim:]
    return jnp.concatenate([first * cosine - second * sine, second * cosine + first * sine], -1)


def window_heads(queries, key_rows, value_rows, visible):
    scale = HD ** (-0.5)

    def one_head(items):
        query_head, key_head, value_head = items
        scores = jnp.dot(query_head, key_head.T, preferred_element_type=jnp.float32) * scale
        scores = jnp.where(visible, scores, -1e30)
        maxima = jnp.max(scores, -1, keepdims=True)
        expo = jnp.exp(scores - maxima)
        weights = (expo / jnp.sum(expo, -1, keepdims=True)).astype(jnp.bfloat16)
        return jnp.dot(weights, value_head, preferred_element_type=jnp.float32).astype(jnp.bfloat16)

    context = lax.map(
        one_head,
        (jnp.moveaxis(queries, 1, 0), jnp.moveaxis(key_rows, 1, 0), jnp.moveaxis(value_rows, 1, 0)),
    )
    return jnp.moveaxis(context, 0, 1)


def body(hidden, proj_weight, stretch_lengths, shard_of):
    states = hidden[0]
    tokens_here = states.shape[0]
    width = proj_weight.shape[2]
    heads_here = width // HD
    seq_index = lax.axis_index("seq")
    group_index = lax.axis_index("index")
    seq_count = lax.axis_size("seq")
    index_count = lax.axis_size("index")
    total_length = tokens_here * seq_count
    positions = seq_index * tokens_here + jnp.arange(tokens_here, dtype=jnp.int32)
    shard_rows = lax.all_gather(proj_weight, "dp", axis=1, tiled=True)
    projected = jnp.einsum(
        "td,jdc->jtc", states, shard_rows[:3], preferred_element_type=jnp.float32
    )
    out_rows_full = shard_rows[3]
    queries = rotate(projected[0].reshape(tokens_here, heads_here, HD), positions).astype(
        jnp.bfloat16
    )
    key_rows = rotate(projected[1].reshape(tokens_here, heads_here, HD), positions).astype(
        jnp.bfloat16
    )
    value_rows = projected[2].astype(jnp.bfloat16)
    stacked = jnp.stack([key_rows.reshape(tokens_here, width), value_rows])
    padded = with_halo(stacked, (("seq", 1),), HALF_WIN)
    span = tokens_here + 2 * HALF_WIN
    key_part = padded[0, 0:span].reshape(span, heads_here, HD)
    value_part = padded[1, 0:span].reshape(span, heads_here, HD)
    key_pos = seq_index * tokens_here + 0 - HALF_WIN + jnp.arange(span, dtype=jnp.int32)
    visible = (
        (jnp.abs(key_pos[None, :] - positions[:, None]) <= HALF_WIN)
        & (key_pos[None, :] >= 0)
        & (key_pos[None, :] < total_length)
    )
    context_parts = window_heads(queries, key_part, value_part, visible).reshape(tokens_here, width)
    partial_value = lax.dot_general(
        context_parts, out_rows_full, (((1,), (1,)), ((), ())), preferred_element_type=jnp.float32
    )
    lengths = stretch_lengths[0]
    stretch_count = lengths.shape[0]
    per_block = stretch_count // seq_count
    ends = jnp.cumsum(lengths, dtype=jnp.int32)
    starts = ends - lengths
    row_ids = jnp.arange(stretch_count, dtype=jnp.int32)
    order = row_ids % per_block * seq_count + row_ids // per_block
    row_starts = starts[order]
    row_ends = ends[order]
    member = (
        (positions[None, :] >= row_starts[:, None]) & (positions[None, :] < row_ends[:, None])
    ).astype(jnp.bfloat16)
    shard_ids = shard_of[0, :, 0]
    local_rows = jnp.arange(per_block, dtype=jnp.int32)
    earlier = (shard_ids[:, None] == shard_ids[None, :]) & (
        local_rows[None, :] < local_rows[:, None]
    )
    slot_rank = jnp.sum(earlier.astype(jnp.int32), 1)
    capacity = per_block // 2
    slot_ids = jnp.arange(capacity, dtype=jnp.int32)
    quarter = D // index_count
    summed = lax.psum_scatter(
        partial_value.astype(jnp.bfloat16), "index", scatter_dimension=1, tiled=True
    ).astype(jnp.float32)
    own_states = lax.dynamic_slice_in_dim(states, group_index * quarter, quarter, 1)
    layer = (own_states.astype(jnp.float32) + summed).astype(jnp.bfloat16)
    partial_pool = jnp.dot(member, layer, preferred_element_type=jnp.float32)
    pooled = lax.psum_scatter(
        partial_pool.astype(jnp.bfloat16), "seq", scatter_dimension=0, tiled=True
    ).astype(jnp.float32)
    shard_range = jnp.arange(index_count, dtype=jnp.int32)
    routing = (
        (shard_ids[None, None, :] == shard_range[:, None, None])
        & (slot_rank[None, None, :] == slot_ids[None, :, None])
    ).astype(jnp.float32)
    outgoing = jnp.einsum("rkc,cf->rkf", routing, pooled, precision=lax.Precision.HIGHEST)
    arrived = lax.all_to_all(outgoing, "index", split_axis=0, concat_axis=2, tiled=True)[0]
    shelf_rows = arrived * lax.rsqrt(jnp.mean(arrived * arrived, -1, keepdims=True) + 1e-06)
    return (layer[None], shelf_rows[None, None, None])


def solution(mesh):
    in_specs = (P("dp", "seq", None), P(None, "dp", "index"), P("dp", None), P("dp", "seq", None))
    out_specs = (P("dp", "seq", "index"), P("dp", "seq", "index", None, None))
    return jax.shard_map(body, mesh=mesh, in_specs=in_specs, out_specs=out_specs, check_vma=False)
```

profile of v0, /device:TPU:32, one launch (start us, length us, event | category | flops | bytes accessed | tf_op | source)
XLA Modules:
  0.0 226.8 jit_solution(12025470082465413667)
XLA Ops:
  7.2 1.9 copy.24
  9.3 1.2 multiply_cosine_fusion
  10.5 116.8 %all-gather.2.cloned.1.call-done = bf16[4,2048,384]{1,2,0:T(8,128)(2,1)} async-done(((bf16[4,128,384]{1,2,0:T(8,128)(2,1)}), bf16[4,2048,384]{1,2,0:T(8,128)(2,1)}) %all-gather.2.cloned.1.call-update) | async-done | bytes 6291472 | tf_op jit(solution)/shard_map/all_gather | solution.py:69
  127.3 4.1 %convolution_bitcast_fusion = f32[3,256,384]{1,2,0:T(8,128)S(1)} fusion(bf16[4,2048,384]{1,2,0:T(8,128)(2,1)} %all-gather.2.cloned.1.call-done, bf16[1,256,2048]{2,1,0:T(8,128)(2,1)} %param.6), kind=kOutput, calls=%fused_computation.24 | convolution fusion | flops 1207959552 | bytes 8519680 | tf_op jit(solution)/shard_map/td,jdc->jtc/dot_general | solution.py:70
  132.6 1.4 subtract_convert_fusion
  134.1 0.4 maximum_bitcast_fusion
  134.7 1.3 collective-permute-start.1
  136.0 3.1 %collective-permute-start = (bf16[2,256,384]{1,2,0:T(8,128)(2,1)S(1)}, bf16[2,256,384]{1,2,0:T(8,128)(2,1)S(1)}, u32[]{:S(2)}, u32[]{:S(2)}) collective-permute-start(bf16[2,256,384]{1,2,0:T(8,128)(2,1)S(1)} %pad_maximum_fusion.2), channel_id=1, source_target_pairs={{0,4},{4,8},{8,12},{12,16},{16,20},{20,24},{24,28},{1,5},{5,9},{9,... | collective-permute-start | bytes 1179656 | tf_op jit(solution)/shard_map/ppermute | solution.py:19
  139.1 1.2 collective-permute-done
  140.6 0.7 copy.30
  141.3 0.7 copy.31
  142.0 7.3 %while.11 = (s32[]{:T(128)}, bf16[6,256,64]{1,2,0:T(8,128)(2,1)S(1)}, bf16[6,256,64]{2,1,0:T(8,128)(2,1)S(1)}, bf16[6,768,64]{2,1,0:T(8,128)(2,1)S(1)}, bf16[6,7...) while((s32[]{:T(128)}, ...), condition=%wide.region_3.4_spmd.clone, body=%wide.region_0.3_spmd.clone.sunk | while | flops 52903424 | bytes 2865261 | solution.py:51
  142.0 0.5 fusion.50
  142.9 0.4 fusion.52
  143.2 0.5 fusion.50
  144.1 0.4 fusion.52
  144.5 0.5 fusion.50
  145.7 0.5 fusion.50
  146.9 0.5 fusion.50
  148.1 0.5 fusion.50
  149.3 3.2 %convolution_convert_fusion.1 = bf16[256,2048]{1,0:T(8,128)(2,1)} fusion(bf16[256,384]{0,1:T(8,128)(2,1)S(1)} %bitcast.86, bf16[4,2048,384]{1,2,0:T(8,128)(2,1)} %all-gather.2.cloned.1.call-done), kind=kOutput, calls=%fused_computation.22 | convolution fusion | flops 403177472 | bytes 2818048 | tf_op jit(solution)/shard_map/dot_general | solution.py:93
  152.8 0.7 gather_fusion.1
  153.5 0.7 gather_fusion
  154.2 1.3 dynamic-slice.1
  156.4 28.2 %reduce-scatter.2.cloned.1.call-done = bf16[256,512]{1,0:T(8,128)(2,1)} async-done(((bf16[256,2048]{1,0:T(8,128)(2,1)}), bf16[256,512]{1,0:T(8,128)(2,1)}) %reduce-scatter.2.cloned.1.call-update) | async-done | bytes 262160 | tf_op jit(solution)/shard_map/reduce_scatter | solution.py:117
  184.6 1.1 convolution_convert_fusion.2
  185.7 24.1 %all-reduce = bf16[32,512]{1,0:T(8,128)(2,1)S(1)} all-reduce(bf16[32,512]{1,0:T(8,128)(2,1)S(1)} %convolution_convert_fusion.2), channel_id=3, replica_groups=mesh['dp'=16,'seq'=8,'index'=4] {'seq'}, use_global_device_ids=true, to_apply=%region_7.8.clone | all-reduce | flops 16384 | bytes 65536
  209.8 0.7 fusion.27
  210.6 3.3 %all-to-all-start = ((f32[4,2,512]{2,1,0:T(2,128)}), f32[4,2,512]{2,1,0:T(2,128)S(1)}, u32[]{:S(2)}, u32[]{:S(2)}) async-start(f32[4,2,512]{2,1,0:T(2,128)} %fusion.27), calls=%async_computation.1 | async-start | bytes 32768 | tf_op jit(solution)/shard_map/all_to_all | solution.py:132
  213.8 1.7 fusion.19
  215.6 3.6 %all-to-all-done = f32[4,2,512]{2,1,0:T(2,128)S(1)} async-done(((f32[4,2,512]{2,1,0:T(2,128)}), f32[4,2,512]{2,1,0:T(2,128)S(1)}, u32[]{:S(2)}, u32[]{:S(2)}) %all-to-all-start) | async-done | bytes 16416 | tf_op jit(solution)/shard_map/all_to_all | solution.py:132
  219.3 0.7 broadcast_multiply_fusion
  (51 shorter events, 5.6 us)
Async XLA Ops:
  7.2 120.1 %all-gather.2.cloned.1.call-start = ((), (), s32[]{:S(2)}) async-start(), calls=%async_computation.2 | async-start | bytes 6684672 | tf_op jit(solution)/shard_map/all_gather | solution.py:69
  9.2 175.4 %reduce-scatter.2.cloned.1.call-start = ((), (), s32[]{:S(2)}) async-start(), calls=%async_computation.3 | async-start | bytes 1310720 | tf_op jit(solution)/shard_map/reduce_scatter | solution.py:117
  134.7 4.4 %collective-permute-start.1 = (bf16[2,256,384]{1,2,0:T(8,128)(2,1)S(1)}, bf16[2,256,384]{1,2,0:T(8,128)(2,1)S(1)}, u32[]{:S(2)}, u32[]{:S(2)}) collective-permute-start(bf16[2,256,384]{1,2,0:T(8,128)(2,1)S(1)} %pad_maximum_fusion.2), channel_id=1, source_target_pairs={{4,0},{8,4},{12,8},{16,12},{20,16},{24,20},{28,24},{5,1},{9,5},{13... | collective-permute-start | bytes 1179656 | tf_op jit(solution)/shard_map/ppermute | solution.py:21
  136.0 4.4 %collective-permute-start = (bf16[2,256,384]{1,2,0:T(8,128)(2,1)S(1)}, bf16[2,256,384]{1,2,0:T(8,128)(2,1)S(1)}, u32[]{:S(2)}, u32[]{:S(2)}) collective-permute-start(bf16[2,256,384]{1,2,0:T(8,128)(2,1)S(1)} %pad_maximum_fusion.2), channel_id=1, source_target_pairs={{0,4},{4,8},{8,12},{12,16},{16,20},{20,24},{24,28},{1,5},{5,9},{9,... | collective-permute-start | bytes 1179656 | tf_op jit(solution)/shard_map/ppermute | solution.py:19
  149.3 3.2 %copy-start.1 = (s32[1,32]{1,0:T(1,128)S(1)}, s32[1,32]{1,0:T(1,128)}, u32[]{:S(2)}) copy-start(s32[1,32]{1,0:T(1,128)} %param.8) | copy-start | bytes 388
  152.5 3.7 %copy-start.2 = (s32[1,4,1]{1,2,0:T(1,128)S(1)}, s32[1,4,1]{1,2,0:T(1,128)}, u32[]{:S(2)}) copy-start(s32[1,4,1]{1,2,0:T(1,128)} %param.9) | copy-start | bytes 52
  152.5 32.1 %copy-start = (bf16[1,256,2048]{2,1,0:T(8,128)(2,1)S(1)}, bf16[1,256,2048]{2,1,0:T(8,128)(2,1)}, u32[]{:S(2)}) copy-start(bf16[1,256,2048]{2,1,0:T(8,128)(2,1)} %param.6) | copy-start | bytes 3145732
  210.6 8.6 %all-to-all-start = ((f32[4,2,512]{2,1,0:T(2,128)}), f32[4,2,512]{2,1,0:T(2,128)S(1)}, u32[]{:S(2)}, u32[]{:S(2)}) async-start(f32[4,2,512]{2,1,0:T(2,128)} %fusion.27), calls=%async_computation.1 | async-start | bytes 32768 | tf_op jit(solution)/shard_map/all_to_all | solution.py:132
Sparse Core Ops, SparseCore 0:
  10.0 117.2 all-gather.1
  152.6 31.8 reduce-scatter.1
where the time goes:
time: 227 us
  waiting for transfers between devices  150 us (66%)
  blocking collectives  24.1 us (11%)
  between operations  15 us (7%)
  matrix products  14.7 us (6%)
  other arithmetic  7.88 us (3%)
  starting transfers between devices  7.68 us (3%)
  local copies, waits for them, and re-layouts  7.61 us (3%)
    all_gather x1, waiting for transfers between devices, body(): shard_rows = lax.all_gather(proj_weight, 'dp', axis=1, tiled=True)  117 us
    reduce_scatter x1, waiting for transfers between devices, body(): lax.psum_scatter(partial_value.astype(jnp.bfloat16), 'index', scatter_dim...  28.2 us
    unnamed x1, blocking collectives  24.1 us
  transfers between devices with their start and end apart: 5, of which 4 were waited for; matrix products, arithmetic and copies ran while one was open for 3% of the time, Pallas kernels for 0%

commit v1 on v0

--- a/solution.py
+++ b/solution.py
@@ -66,7 +66,10 @@
     index_count = lax.axis_size("index")
     total_length = tokens_here * seq_count
     positions = seq_index * tokens_here + jnp.arange(tokens_here, dtype=jnp.int32)
-    shard_rows = lax.all_gather(proj_weight, "dp", axis=1, tiled=True)
+    n_dev = lax.axis_size("dp")
+    shards = jnp.stack([proj_weight for _ in range(n_dev)])
+    shards = lax.all_to_all(shards, "dp", split_axis=0, concat_axis=0)
+    shard_rows = jnp.concatenate(shards, axis=1)
     projected = jnp.einsum(
         "td,jdc->jtc", states, shard_rows[:3], preferred_element_type=jnp.float32
     )

time: 227 us -> 420 us (1.85)
  waiting for transfers between devices: 150 us -> 308 us
  local copies, waits for them, and re-layouts: 7.61 us -> 24.9 us
  starting transfers between devices: 7.68 us -> 21.1 us
    all_to_all x0 -> x1, waiting for transfers between devices: none -> 272 us  [body(): shards = lax.all_to_all(shards, 'dp', split_axis=0, concat_axis=0)]
    all_gather x1 -> x0, waiting for transfers between devices: 117 us -> none  [body(): shard_rows = lax.all_gather(proj_weight, 'dp', axis=1, tiled=True)]
    all_to_all x0 -> x1, starting transfers between devices: none -> 15.2 us  [body(): shards = lax.all_to_all(shards, 'dp', split_axis=0, concat_axis=0)]
    all_to_all x0 -> x1, local copies, waits for them, and re-layouts: none -> 8.66 us  [body(): shards = lax.all_to_all(shards, 'dp', split_axis=0, concat_axis=0)]
    dot_general x6, matrix products: 3.23 us -> 9 us  [one_head(): jnp.dot(query_head, key_head.T, preferred_element_type=jnp.float32) * scale]
    slice x0 -> x2, local copies, waits for them, and re-layouts: none -> 4.57 us  [the longest x1 2.9 us: body(): shard_rows[:3]]
  transfers between devices with their start and end apart: 5 -> 5, of which waited for: 4 -> 4; matrix products, arithmetic and copies ran while one was open for 3% -> 2% of each run, Pallas kernels for 0% -> 0%
where the time goes in v1:
time: 420 us; the launch traced here: 419 us
  waiting for transfers between devices  308 us (73%)
  local copies, waits for them, and re-layouts  24.9 us (6%)
  blocking collectives  24 us (6%)
  starting transfers between devices  21.1 us (5%)
  matrix products  16.4 us (4%)
  between operations  15 us (4%)
  other arithmetic  9.51 us (2%)
    all_to_all x1, waiting for transfers between devices, body(): shards = lax.all_to_all(shards, 'dp', split_axis=0, concat_axis=0)  272 us
    reduce_scatter x1, waiting for transfers between devices, body(): lax.psum_scatter(partial_value.astype(jnp.bfloat16), 'index', scatter_dim...  31.8 us
    unnamed x1, blocking collectives  24 us
    all_to_all x1, starting transfers between devices, body(): shards = lax.all_to_all(shards, 'dp', split_axis=0, concat_axis=0)  15.2 us
    dot_general x6, matrix products, one_head(): jnp.dot(query_head, key_head.T, preferred_element_type=jnp.float32) * scale  9 us
    all_to_all x1, local copies, waits for them, and re-layouts, body(): shards = lax.all_to_all(shards, 'dp', split_axis=0, concat_axis=0)  8.66 us
  transfers between devices with their start and end apart: 5, of which 4 were waited for; matrix products, arithmetic and copies ran while one was open for 2% of the time, Pallas kernels for 0%

profile of v1, /device:TPU:32, one launch (start us, length us, event | category | flops | bytes accessed | tf_op | source)
XLA Modules:
  0.0 419.3 jit_solution(1898351370210237286)
XLA Ops:
  7.2 1.2 copy.35
  8.4 4.2 stack.4
  12.6 15.2 %all-to-all-start = ((bf16[16,4,128,384]{2,3,1,0:T(8,128)(2,1)}), bf16[16,4,128,384]{2,3,1,0:T(8,128)(2,1)}, u32[]{:S(2)}, u32[]{:S(2)}) async-start(bf16[16,4,128,384]{2,3,1,0:T(8,128)(2,1)} %stack.4), calls=%async_computation | async-start | bytes 12582912 | tf_op jit(solution)/shard_map/all_to_all | solution.py:71
  27.8 1.2 multiply_cosine_fusion
  29.1 271.7 %all-to-all-done = bf16[16,4,128,384]{2,3,1,0:T(8,128)(2,1)} async-done(((bf16[16,4,128,384]{2,3,1,0:T(8,128)(2,1)}), bf16[16,4,128,384]{2,3,1,0:T(8,128)(2,1)}, u32[]{:S(2)}, u32[]{:S(2)}) %all-to-all-start) | async-done | bytes 6291488 | tf_op jit(solution)/shard_map/all_to_all | solution.py:71
  300.7 8.7 %copy.36 = bf16[16,4,128,384]{3,2,0,1:T(8,128)(2,1)} copy(bf16[16,4,128,384]{2,3,1,0:T(8,128)(2,1)} %all-to-all-done) | data formatting | bytes 12582912 | tf_op jit(solution)/shard_map/all_to_all | solution.py:71
  309.4 2.9 slice.54
  312.3 1.4 convolution_bitcast_fusion
  315.0 2.3 subtract_convert_fusion
  317.8 1.3 collective-permute-start
  319.1 1.3 collective-permute-start.1
  320.4 1.7 slice.64
  322.1 1.0 maximum_bitcast_fusion
  323.1 1.3 collective-permute-done.1
  324.6 1.4 copy.43
  325.9 0.7 copy.44
  326.7 13.0 %while.11 = (s32[]{:T(128)}, bf16[6,256,64]{1,2,0:T(8,128)(2,1)S(1)}, bf16[6,256,64]{2,1,0:T(8,128)(2,1)}, bf16[6,768,64]{2,1,0:T(8,128)(2,1)}, bf16[6,768,64]{2...) while((s32[]{:T(128)}, ...), condition=%wide.region_3.4_spmd.clone, body=%wide.region_0.3_spmd.clone.sunk | while | flops 52903424 | bytes 2863717 | solution.py:51
  326.7 1.5 fusion.51
  328.8 1.5 fusion.51
  331.0 1.5 fusion.51
  333.2 1.5 fusion.51
  335.4 1.5 fusion.51
  337.5 1.5 fusion.51
  339.7 1.7 convolution_convert_fusion.1
  343.2 1.3 dynamic-slice.1
  345.4 31.8 %reduce-scatter.2.cloned.1.call-done = bf16[256,512]{1,0:T(8,128)(2,1)} async-done(((bf16[256,2048]{1,0:T(8,128)(2,1)}), bf16[256,512]{1,0:T(8,128)(2,1)}) %reduce-scatter.2.cloned.1.call-update) | async-done | bytes 262160 | tf_op jit(solution)/shard_map/reduce_scatter | solution.py:120
  377.2 1.1 convolution_convert_fusion.2
  378.3 24.0 %all-reduce = bf16[32,512]{1,0:T(8,128)(2,1)S(1)} all-reduce(bf16[32,512]{1,0:T(8,128)(2,1)S(1)} %convolution_convert_fusion.2), channel_id=3, replica_groups=mesh['dp'=16,'seq'=8,'index'=4] {'seq'}, use_global_device_ids=true, to_apply=%region_7.8.clone | all-reduce | flops 16384 | bytes 65536
  402.3 0.7 fusion.27
  403.1 3.3 all-to-all-start.1
  406.3 1.7 fusion.19
  408.1 3.6 all-to-all-done.1
  (60 shorter events, 8.6 us)
Async XLA Ops:
  12.6 288.2 %all-to-all-start = ((bf16[16,4,128,384]{2,3,1,0:T(8,128)(2,1)}), bf16[16,4,128,384]{2,3,1,0:T(8,128)(2,1)}, u32[]{:S(2)}, u32[]{:S(2)}) async-start(bf16[16,4,128,384]{2,3,1,0:T(8,128)(2,1)} %stack.4), calls=%async_computation | async-start | bytes 12582912 | tf_op jit(solution)/shard_map/all_to_all | solution.py:71
  27.8 349.4 %reduce-scatter.2.cloned.1.call-start = ((), (), s32[]{:S(2)}) async-start(), calls=%async_computation.3 | async-start | bytes 1310720 | tf_op jit(solution)/shard_map/reduce_scatter | solution.py:120
  309.4 2.9 copy-start.2
  317.8 5.4 %collective-permute-start = (bf16[2,256,384]{1,2,0:T(8,128)(2,1)S(1)}, bf16[2,256,384]{1,2,0:T(8,128)(2,1)S(1)}, u32[]{:S(2)}, u32[]{:S(2)}) collective-permute-start(bf16[2,256,384]{1,2,0:T(8,128)(2,1)S(1)} %pad_maximum_fusion.2), channel_id=1, source_target_pairs={{0,4},{4,8},{8,12},{12,16},{16,20},{20,24},{24,28},{1,5},{5,9},{9,... | collective-permute-start | bytes 1179656 | tf_op jit(solution)/shard_map/ppermute | solution.py:19
  319.1 5.3 %collective-permute-start.1 = (bf16[2,256,384]{1,2,0:T(8,128)(2,1)S(1)}, bf16[2,256,384]{1,2,0:T(8,128)(2,1)S(1)}, u32[]{:S(2)}, u32[]{:S(2)}) collective-permute-start(bf16[2,256,384]{1,2,0:T(8,128)(2,1)S(1)} %pad_maximum_fusion.2), channel_id=1, source_target_pairs={{4,0},{8,4},{12,8},{16,12},{20,16},{24,20},{28,24},{5,1},{9,5},{13... | collective-permute-start | bytes 1179656 | tf_op jit(solution)/shard_map/ppermute | solution.py:21
  320.4 1.7 copy-start
  320.4 1.7 copy-start.1
  339.7 1.8 copy-start.4
  341.5 3.7 copy-start.5
  341.5 35.7 %copy-start.3 = (bf16[1,256,2048]{2,1,0:T(8,128)(2,1)S(1)}, bf16[1,256,2048]{2,1,0:T(8,128)(2,1)}, u32[]{:S(2)}) copy-start(bf16[1,256,2048]{2,1,0:T(8,128)(2,1)} %param.6) | copy-start | bytes 3145732
  403.1 8.6 %all-to-all-start.1 = ((f32[4,2,512]{2,1,0:T(2,128)}), f32[4,2,512]{2,1,0:T(2,128)S(1)}, u32[]{:S(2)}, u32[]{:S(2)}) async-start(f32[4,2,512]{2,1,0:T(2,128)} %fusion.27), calls=%async_computation.2 | async-start | bytes 32768 | tf_op jit(solution)/shard_map/all_to_all | solution.py:135
Sparse Core Ops, SparseCore 0:
  341.6 35.5 reduce-scatter.1
